TPU v7x, 32 devices: a whole 2x2x4 slice. The times are simulated.
32 devices in a mesh: seq: 4 (over y, x), grp: 8 (over z, core).
Axes of the slice: x: 2, y: 2, z: 4, core: 2. Of those that a mesh axis runs over, the one named last changes fastest.
Arguments:
- tokens: bfloat16 [16384, 768], P(('grp', 'seq')), may hold values from -6 to 6
- cotangent: bfloat16 [16384, 768], P(('grp', 'seq')), may hold values from -6 to 6
- seq_len: int32 [8], P('grp'), may hold values from 1024 to 2048, as said below
- weight_mats: bfloat16 [768, 9280], replicated
- weight_vecs: bfloat16 [768, 13], replicated
- master_mats: float32 [768, 9280], P('grp'), may hold values from -0.21875 to 0.21875
- master_vecs: float32 [768, 13], P('grp'), may hold values from -3 to 3
- moment_mats: float32 [768, 9280], P('grp'), may hold values from -384 to 384
- moment_vecs: float32 [768, 13], P('grp'), may hold values from -384 to 384
- square_mats: float32 [768, 9280], P('grp'), may hold values from 819.2 to 32768
- square_vecs: float32 [768, 13], P('grp'), may hold values from 819.2 to 32768
- average_mats: float32 [768, 9280], P('grp'), may hold values from -0.21875 to 0.21875
- average_vecs: float32 [768, 13], P('grp'), may hold values from -3 to 3
Outputs:
- block_output: bfloat16 [16384, 768], P(('grp', 'seq'))
- input_grad: bfloat16 [16384, 768], P(('grp', 'seq'))
- grad_mats: float32 [768, 9280], P('grp')
- grad_vecs: float32 [768, 13], P('grp')
- master_mats_new: float32 [768, 9280], P('grp')
- master_vecs_new: float32 [768, 13], P('grp')
- moment_mats_new: float32 [768, 9280], P('grp')
- moment_vecs_new: float32 [768, 13], P('grp')
- square_mats_new: float32 [768, 9280], P('grp')
- square_vecs_new: float32 [768, 13], P('grp')
- average_mats_new: float32 [768, 9280], P('grp')
- average_vecs_new: float32 [768, 13], P('grp')
- copy_mats: bfloat16 [768, 9280], P('grp')
- copy_vecs: bfloat16 [768, 13], P('grp')
Inputs may be any that keep to these rules, and one draw needn't show every extreme that they name: Each group's sequences all have the length seq_len of that group; both values 2 * 512 and 2048 occur in every draw.
All inputs are finite; a program needn't handle non-finite values.
Results may differ from a plain program's by a relative error of at most 0.018.
Values may be sent and summed in bfloat16 or wider, within the bound.
No kernel may reach another device: no remote copies, remote signals or barrier semaphores. Data moves between devices by JAX's collectives and lax.ppermute only.
A program may use at most 192 MiB of HBM per device.

v0:
```python
from functools import partial
import jax
import jax.numpy as jnp
from jax import lax
from jax.sharding import PartitionSpec as P

D = 768
HEADS = 12
HD = 64
FF = 3072
norm_eps = 1e-05
adam_eps = 1e-08
beta_first = 0.5
beta_second = 0.5
learn_rate = 0.01
vector_rate = 0.06
decay_rate = 0.1
average_keep = 0.9
highest = lax.Precision.HIGHEST
careful_level = lax.Precision.HIGH


def contract_rows(left, right):
    return lax.dot_general(
        left, right, (((0,), (0,)), ((), ())), preferred_element_type=jnp.float32
    )


def contract_cols(left, right):
    return lax.dot_general(
        left, right, (((1,), (1,)), ((), ())), preferred_element_type=jnp.float32
    )


def precise(left, right):
    return jnp.dot(left, right, preferred_element_type=jnp.float32, precision=careful_level)


def norm_rows(values, gain, shift):
    average = jnp.mean(values, axis=1, keepdims=True)
    centered = values - average
    variance = jnp.mean(centered * centered, axis=1, keepdims=True)
    return centered * lax.rsqrt(variance + norm_eps) * gain + shift


def norm_back(values, gain, upstream):
    average = jnp.mean(values, axis=1, keepdims=True)
    centered = values - average
    variance = jnp.mean(centered * centered, axis=1, keepdims=True)
    inverse = lax.rsqrt(variance + norm_eps)
    normed = centered * inverse
    d_gain = jnp.sum(upstream * normed, axis=0)
    d_shift = jnp.sum(upstream, axis=0)
    d_normed = upstream * gain
    d_values = inverse * (
        d_normed
        - jnp.mean(d_normed, axis=1, keepdims=True)
        - normed * jnp.mean(d_normed * normed, axis=1, keepdims=True)
    )
    return (d_values, d_gain, d_shift)


def feature_map(values, hedge_map):
    count = values.shape[0]
    per_head = values.reshape(count, HEADS, HD)
    scores = jnp.einsum("nhi,hij->nhj", per_head, hedge_map, precision=highest)
    return jnp.concatenate(
        [jax.nn.softmax(scores, axis=-1), jax.nn.softmax(-scores, axis=-1)], axis=-1
    )


def adam_step(grad, master, first, second, rate):
    new_first = beta_first * first + (1.0 - beta_first) * grad
    new_second = beta_second * second + (1.0 - beta_second) * grad * grad
    new_master = master - rate * (
        new_first / (jnp.sqrt(new_second) + adam_eps) + decay_rate * master
    )
    return (new_master, new_first, new_second)


def on_device(
    tokens,
    cotangent,
    seq_len,
    weight_mats,
    weight_vecs,
    master_mats,
    master_vecs,
    moment_mats,
    moment_vecs,
    square_mats,
    square_vecs,
    average_mats,
    average_vecs,
):
    rows = tokens.shape[0]
    my_start = lax.axis_index("seq") * rows
    seq_length = seq_len[0]
    starts = (my_start % seq_length == 0).astype(jnp.float32)
    continued = 1.0 - starts
    w_qkv = weight_mats[:, : 3 * D]
    w_proj = weight_mats[:, 3 * D : 4 * D]
    w_fc = weight_mats[:, 4 * D : 4 * D + FF]
    w_down = weight_mats[:, 4 * D + FF : 4 * D + 2 * FF]
    hedge_map = weight_mats[:, 4 * D + 2 * FF :].astype(jnp.float32).reshape(HEADS, HD, HD)
    vec_all = weight_vecs.astype(jnp.float32)
    gain_one = vec_all[:, 0]
    gain_two = vec_all[:, 2]
    bias_qkv = vec_all[:, 6:9].T.reshape(3 * D)
    bias_fc = vec_all[:, 9:].T.reshape(FF)
    line_index = jnp.arange(rows, dtype=jnp.int32)
    causal = (line_index[:, None] >= line_index[None, :]).astype(jnp.float32)
    inputs = tokens.astype(jnp.float32)
    normed_low = norm_rows(inputs, gain_one, vec_all[:, 1]).astype(jnp.bfloat16)
    projected = jnp.dot(normed_low, w_qkv, preferred_element_type=jnp.float32) + bias_qkv
    queries = projected[:, :D]
    keys = projected[:, D : 2 * D]
    values_low = projected[:, 2 * D :].astype(jnp.bfloat16)
    query_full, query_back = jax.vjp(feature_map, queries, hedge_map)
    key_full, key_back = jax.vjp(feature_map, keys, hedge_map)
    query_feat = query_full.astype(jnp.bfloat16)
    key_feat = key_full.astype(jnp.bfloat16)
    value_heads = values_low.reshape(rows, HEADS, HD)
    gath_keys, gath_values = (
        lax.all_gather(key_feat.reshape(rows, 2 * D), "seq", axis=0, tiled=True),
        lax.all_gather(values_low, "seq", axis=0, tiled=True),
    )
    positions = jnp.arange(gath_keys.shape[0], dtype=jnp.int32)
    keep_rows = (
        (positions < my_start) & (positions // seq_length == my_start // seq_length)
    ).astype(jnp.bfloat16)
    kept_keys = (gath_keys * keep_rows[:, None]).reshape(-1, HEADS, 2 * HD)
    state_in = jnp.einsum(
        "nhf,nhd->hfd",
        kept_keys,
        gath_values.reshape(-1, HEADS, HD),
        preferred_element_type=jnp.float32,
    )
    total_in = jnp.sum(kept_keys, axis=0, dtype=jnp.float32)
    query_heads = jnp.transpose(query_feat, (1, 0, 2))
    key_heads = jnp.transpose(key_feat, (1, 0, 2))
    value_major = jnp.transpose(value_heads, (1, 0, 2))

    def attend(parts):
        query_part, key_part, value_part, state, total = parts
        query_wide = query_part.astype(jnp.float32)
        weights = jnp.dot(query_part, key_part.T, preferred_element_type=jnp.float32) * causal
        numer = precise(weights, value_part.astype(jnp.float32)) + precise(query_wide, state)
        denom = jnp.sum(weights, axis=1) + precise(query_wide, total)
        return (numer / denom[:, None], denom)

    head_outs, denoms = lax.map(attend, (query_heads, key_heads, value_major, state_in, total_in))
    mixed_low = jnp.transpose(head_outs, (1, 0, 2)).reshape(rows, D).astype(jnp.bfloat16)
    attn_out = jnp.dot(mixed_low, w_proj, preferred_element_type=jnp.float32) + vec_all[:, 4]
    resid = inputs + attn_out
    normed_two_low = norm_rows(resid, gain_two, vec_all[:, 3]).astype(jnp.bfloat16)
    hidden_pre = jnp.dot(normed_two_low, w_fc, preferred_element_type=jnp.float32) + bias_fc
    hidden_act, gelu_back = jax.vjp(partial(jax.nn.gelu, approximate=True), hidden_pre)
    hidden_low = hidden_act.astype(jnp.bfloat16)
    result = resid + contract_cols(hidden_low, w_down) + vec_all[:, 5]
    block_output = result.astype(jnp.bfloat16)
    grad_out = cotangent.astype(jnp.float32)
    d_down = contract_rows(cotangent, hidden_low)
    d_bias_down = jnp.sum(grad_out, axis=0)
    d_hidden = jnp.dot(cotangent, w_down, preferred_element_type=jnp.float32)
    d_pre_low = gelu_back(d_hidden)[0].astype(jnp.bfloat16)
    d_fc = contract_rows(normed_two_low, d_pre_low)
    d_bias_fc = jnp.sum(d_pre_low.astype(jnp.float32), axis=0)
    d_normed_two = contract_cols(d_pre_low, w_fc)
    d_resid_norm, d_gain_two, d_shift_two = norm_back(resid, gain_two, d_normed_two)
    d_resid = grad_out + d_resid_norm
    d_attn_low = d_resid.astype(jnp.bfloat16)
    d_bias_proj = jnp.sum(d_attn_low.astype(jnp.float32), axis=0)
    d_proj = contract_rows(mixed_low, d_attn_low)
    d_mixed_low = lax.optimization_barrier(contract_cols(d_attn_low, w_proj).astype(jnp.bfloat16))
    d_mixed = jnp.transpose(d_mixed_low.astype(jnp.float32).reshape(rows, HEADS, HD), (1, 0, 2))

    def attend_back(parts):
        query_part, key_part, value_part, state, total, outs, denom, upstream = parts
        query_wide = query_part.astype(jnp.float32)
        key_wide = key_part.astype(jnp.float32)
        weights = jnp.dot(query_part, key_part.T, preferred_element_type=jnp.float32) * causal
        ratio = upstream / denom[:, None]
        offset = -jnp.sum(upstream * outs, axis=1) / denom
        d_weights = (precise(ratio, value_part.astype(jnp.float32).T) + offset[:, None]) * causal
        d_query = (
            precise(d_weights, key_wide)
            + precise(ratio, state.T)
            + offset[:, None] * total[None, :]
        )
        d_key = precise(d_weights.T, query_wide)
        d_value = precise(weights.T, ratio)
        back_state = precise(query_wide.T, ratio) * continued
        back_total = precise(offset, query_wide) * continued
        return (d_query, d_key, d_value, back_state, back_total)

    d_query_h, d_key_h, d_value_h, back_state, back_total = lax.map(
        attend_back,
        (query_heads, key_heads, value_major, state_in, total_in, head_outs, denoms, d_mixed),
    )
    count = rows * lax.axis_size("seq")
    keys_part = gath_keys.astype(jnp.float32).reshape(count, HEADS, 2 * HD)
    vals_part = gath_values.astype(jnp.float32).reshape(count, HEADS, HD)
    keep_part = keep_rows.astype(jnp.float32)
    d_keys_part = (
        jnp.einsum("nhd,hfd->nhf", vals_part, back_state, precision=careful_level)
        + back_total[None]
    ) * keep_part[:, None, None]
    d_vals_part = (
        jnp.einsum("nhf,hfd->nhd", keys_part, back_state, precision=careful_level)
        * keep_part[:, None, None]
    )
    remote = lax.psum_scatter(
        jnp.concatenate(
            [d_keys_part.reshape(count, 2 * D), d_vals_part.reshape(count, D)], axis=1
        ).astype(jnp.bfloat16),
        "seq",
        scatter_dimension=0,
        tiled=True,
    ).astype(jnp.float32)
    d_key_extra = remote[:, : 2 * D].reshape(rows, HEADS, 2 * HD)
    d_value_extra = remote[:, 2 * D :].reshape(rows, HEADS, HD)
    d_query_all = jnp.transpose(d_query_h, (1, 0, 2))
    d_key_all = jnp.transpose(d_key_h, (1, 0, 2)) + d_key_extra
    d_value_all = jnp.transpose(d_value_h, (1, 0, 2)) + d_value_extra
    d_queries, d_map_query = query_back(d_query_all)
    d_keys, d_map_key = key_back(d_key_all)
    d_proj_low = jnp.concatenate([d_queries, d_keys, d_value_all.reshape(rows, D)], axis=1).astype(
        jnp.bfloat16
    )
    d_qkv = contract_rows(normed_low, d_proj_low)
    d_bias_qkv = jnp.sum(d_proj_low.astype(jnp.float32), axis=0)
    d_normed_one = contract_cols(d_proj_low, w_qkv)
    d_input_norm, d_gain_one, d_shift_one = norm_back(inputs, gain_one, d_normed_one)
    input_grad = (d_resid + d_input_norm).astype(jnp.bfloat16)
    grad_mats = jnp.concatenate(
        [d_qkv, d_proj, d_fc, d_down, (d_map_query + d_map_key).reshape(D, HD)], axis=1
    )
    grad_vecs = jnp.concatenate(
        [
            jnp.stack(
                [d_gain_one, d_shift_one, d_gain_two, d_shift_two, d_bias_proj, d_bias_down], axis=1
            ),
            d_bias_qkv.reshape(3, D).T,
            d_bias_fc.reshape(FF // D, D).T,
        ],
        axis=1,
    )
    owned_mats, owned_vecs = (
        lax.psum_scatter(grad_mats, "grp", scatter_dimension=0, tiled=True),
        lax.psum_scatter(grad_vecs, "grp", scatter_dimension=0, tiled=True),
    )
    grad_mats_own, grad_vecs_own = (
        lax.psum(owned_mats.astype(jnp.bfloat16), "seq").astype(jnp.float32),
        lax.psum(owned_vecs.astype(jnp.bfloat16), "seq").astype(jnp.float32),
    )
    new_mats, new_first_m, new_second_m = adam_step(
        grad_mats_own, master_mats, moment_mats, square_mats, learn_rate
    )
    new_vecs, new_first_v, new_second_v = adam_step(
        grad_vecs_own, master_vecs, moment_vecs, square_vecs, vector_rate
    )
    new_avg_m = average_keep * average_mats + (1.0 - average_keep) * new_mats
    new_avg_v = average_keep * average_vecs + (1.0 - average_keep) * new_vecs
    return (
        block_output,
        input_grad,
        grad_mats_own,
        grad_vecs_own,
        new_mats,
        new_vecs,
        new_first_m,
        new_first_v,
        new_second_m,
        new_second_v,
        new_avg_m,
        new_avg_v,
        new_mats.astype(jnp.bfloat16),
        new_vecs.astype(jnp.bfloat16),
    )


def solution(mesh):
    in_specs = (
        P(("grp", "seq"), None),
        P(("grp", "seq"), None),
        P("grp"),
        P(),
        P(),
        P("grp", None),
        P("grp", None),
        P("grp", None),
        P("grp", None),
        P("grp", None),
        P("grp", None),
        P("grp", None),
        P("grp", None),
    )
    out_specs = (
        P(("grp", "seq"), None),
        P(("grp", "seq"), None),
        P("grp", None),
        P("grp", None),
        P("grp", None),
        P("grp", None),
        P("grp", None),
        P("grp", None),
        P("grp", None),
        P("grp", None),
        P("grp", None),
        P("grp", None),
        P("grp", None),
        P("grp", None),
    )
    return jax.shard_map(
        on_device, mesh=mesh, in_specs=in_specs, out_specs=out_specs, check_vma=False
    )
```

profile of v0, /device:TPU:0, one launch (start us, length us, event | category | flops | bytes accessed | tf_op | source)
XLA Modules:
  0.0 1010.2 jit_solution(10283826518961896790)
XLA Ops:
  11.6 4.2 convolution_add_fusion.3
  19.1 3.3 fusion.162
  25.0 2.4 fusion.165
  45.7 3.1 copy.80
  50.2 2.6 copy.81
  53.0 12.7 %all-gather.5.cloned.1.call-done = bf16[2048,768]{1,0:T(8,128)(2,1)} async-done(((bf16[512,768]{1,0:T(8,128)(2,1)}), bf16[2048,768]{1,0:T(8,128)(2,1)}) %all-gather.5.cloned.1.call-update) | async-done | bytes 3145744 | tf_op jit(solution)/shard_map/all_gather | solution.py:126
  65.8 4.6 copy.78
  70.4 67.8 %all-gather.3.cloned.1.call-done = bf16[2048,1536]{0,1:T(8,128)(2,1)} async-done(((bf16[512,1536]{0,1:T(8,128)(2,1)}), bf16[2048,1536]{0,1:T(8,128)(2,1)}) %all-gather.3.cloned.1.call-update) | async-done | bytes 6291472 | tf_op jit(solution)/shard_map/all_gather | solution.py:125
  138.2 5.0 convert_reduce_fusion
  146.4 81.3 %while.33 = (s32[]{:T(128)}, f32[12,512,64]{1,2,0:T(8,128)}, f32[12,512]{1,0:T(8,128)}, bf16[12,512,128]{2,1,0:T(8,128)(2,1)}, bf16[12,512,128]{2,1,0:T(8,128)(2...) while((s32[]{:T(128)}, f32[12,512,64]{1,2,0:T(8,128)}, ...), condition=%wide.region_13.14_spmd.clone, body=%wide.region_11.13_spmd.clone.sunk | while | flops 194183168 | bytes 3231861 | solution.py:152
  229.5 2.4 fusion.167
  232.4 5.0 fusion.85
  237.4 11.5 %convert_reduce_fusion.1 = (f32[3072]{0:T(1024)}, bf16[512,3072]{1,0:T(8,128)(2,1)S(1)}) fusion(f32[512,3072]{1,0:T(8,128)S(1)} %fusion.85, f32[3072]{0:T(1024)S(1)} %add.216, bf16[512,768]{1,0:T(8,128)(2,1)S(1)} %copy-done.40, bf16[768,9280]{0,1:T(8,128)(2,1)} %param.20), kind=kOutput, calls=%fused_computation.105 | convolution fusion | flops 2452091904 | bytes 14966784 | tf_op jit(solution)/shard_map/dot_general | solution.py:165
  249.0 3.5 multiply_reduce_fusion
  258.5 202.7 %while.34 = (s32[]{:T(128)}, f32[12,512,128]{1,2,0:T(8,128)}, f32[12,512,128]{1,2,0:T(8,128)}, f32[12,512,64]{1,2,0:T(8,128)}, f32[12,128,64]{1,2,0:T(8,128)}, /...) while((s32[]{:T(128)}, f32[12,512,128]{1,2,0:T(8,128)}, ...), condition=%wide.region_20.21_spmd.clone.clone, body=%wide.region_18.20_spmd.clone.clone.sunk | while | flops 723526784 | bytes 10363109 | solution.py:197
  461.3 5.1 multiply_convert_fusion.1
  466.4 5.4 multiply_convert_fusion
  471.8 11.6 %pad_maximum_fusion = bf16[2048,2304]{0,1:T(8,128)(2,1)} fusion(bf16[2048,768]{0,1:T(8,128)(2,1)S(1)} %bitcast.307, bf16[2048,1536]{0,1:T(8,128)(2,1)S(1)} %bitcast.302), kind=kLoop, calls=%fused_computation.92 | loop fusion | flops 18874368 | bytes 18874368 | tf_op jit(solution)/shard_map/concatenate | solution.py:214
  484.8 3.4 multiply_reduce_fusion.4
  491.5 87.1 %reduce-scatter.6.cloned.1.call-done = bf16[512,2304]{0,1:T(8,128)(2,1)} async-done(((bf16[2048,2304]{0,1:T(8,128)(2,1)}), bf16[512,2304]{0,1:T(8,128)(2,1)}) %reduce-scatter.6.cloned.1.call-update) | async-done | bytes 2359312 | tf_op jit(solution)/shard_map/reduce_scatter | solution.py:213
  592.2 5.4 convolution_dynamic-update-slice_fusion
  600.0 5.5 convolution_dynamic-update-slice_fusion.1
  605.5 5.5 bitcast_dynamic-update-slice_fusion
  614.4 6.0 fusion.110
  621.8 270.7 %reduce-scatter.8.cloned.1.call-done = f32[96,9280]{1,0:T(8,128)} async-done(((f32[768,9280]{1,0:T(8,128)}), f32[96,9280]{1,0:T(8,128)}) %reduce-scatter.8.cloned.1.call-update) | async-done | bytes 3563536 | tf_op jit(solution)/shard_map/reduce_scatter | solution.py:250
  892.5 3.4 convert_element_type.146
  896.6 9.6 add_convert_fusion
  907.7 16.4 %reduce-scatter.10.cloned.1.call-done = f32[96,13]{1,0:T(8,128)} async-done(((f32[768,13]{1,0:T(8,128)}), f32[96,13]{1,0:T(8,128)}) %reduce-scatter.10.cloned.1.call-update) | async-done | bytes 5008
  925.0 10.0 psum.15
  936.3 54.8 %all-reduce.2.cloned.1.call-done = bf16[96,9280]{1,0:T(8,128)(2,1)} async-done(((bf16[96,9280]{1,0:T(8,128)(2,1)}), bf16[96,9280]{1,0:T(8,128)(2,1)}) %all-reduce.2.cloned.1.call-update) | async-done | bytes 1781776 | tf_op jit(solution)/shard_map/psum | solution.py:254
  991.1 8.9 fusion.158
  1000.1 2.8 multiply_add_fusion.1
  (577 shorter events, 353.1 us)
Async XLA Ops:
  7.2 58.6 %all-gather.5.cloned.1.call-start = ((), (), s32[]{:S(2)}) async-start(), calls=%async_computation.4 | async-start | bytes 3932160 | tf_op jit(solution)/shard_map/all_gather | solution.py:126
  8.7 7.1 copy-start.53
  8.7 7.1 copy-start.71
  8.7 223.7 %copy-start.69 = (f32[768]{0:T(1024)}, f32[768]{0:T(1024)S(1)}, u32[]{:S(2)}) copy-start(f32[768]{0:T(1024)S(1)} %get-tuple-element.327) | copy-start | bytes 9220
  8.7 243.8 %copy-start.51 = (f32[768]{0:T(1024)}, f32[768]{0:T(1024)S(1)}, u32[]{:S(2)}) copy-start(f32[768]{0:T(1024)S(1)} %get-tuple-element.325) | copy-start | bytes 9220
  10.0 5.7 copy-start.45
  18.9 119.3 %all-gather.3.cloned.1.call-start = ((), (), s32[]{:S(2)}) async-start(), calls=%async_computation.3 | async-start | bytes 7864320 | tf_op jit(solution)/shard_map/all_gather | solution.py:125
  19.1 18.3 %copy-start.30 = (bf16[768,64]{1,0:T(8,128)(2,1)}, bf16[768,64]{1,0:T(8,128)(2,1)S(1)}, u32[]{:S(2)}) copy-start(bf16[768,64]{1,0:T(8,128)(2,1)S(1)} %copy.136) | copy-start | bytes 294916
  32.5 546.0 %reduce-scatter.6.cloned.1.call-start = ((), (), s32[]{:S(2)}) async-start(), calls=%async_computation.5 | async-start | bytes 11796480 | tf_op jit(solution)/shard_map/reduce_scatter | solution.py:213
  34.0 203.4 %copy-start.55 = (f32[3072]{0:T(1024)}, f32[3072]{0:T(1024)S(1)}, u32[]{:S(2)}) copy-start(f32[3072]{0:T(1024)S(1)} %add.216) | copy-start | bytes 36868
  232.0 20.5 %copy-start.27 = (f32[512,768]{1,0:T(8,128)}, f32[512,768]{1,0:T(8,128)S(1)}, u32[]{:S(2)}) copy-start(f32[512,768]{1,0:T(8,128)S(1)} %get-tuple-element.409) | copy-start | bytes 4718596
  232.0 20.5 %copy-start.47 = (f32[512]{0:T(512)}, f32[512]{0:T(512)S(1)}, u32[]{:S(2)}) copy-start(f32[512]{0:T(512)S(1)} %broadcast_multiply_fusion.5) | copy-start | bytes 6148
  232.3 20.2 %copy-start.60 = (f32[512]{0:T(512)}, f32[512]{0:T(512)S(1)}, u32[]{:S(2)}) copy-start(f32[512]{0:T(512)S(1)} %add_rsqrt_fusion) | copy-start | bytes 6148
  232.4 16.6 %slice-start = ((s8[14254080]{0:T(1024)(128)(4,1)}), s8[4194304]{0:T(1024)(128)(4,1)S(1)}, s32[]{:S(2)}) async-start(s8[14254080]{0:T(1024)(128)(4,1)} %bitcast.338), calls=%async_computation.9 | async-start | bytes 8388608
  232.4 16.6 %slice-start.1 = ((s8[14254080]{0:T(1024)(128)(4,1)}), s8[4194304]{0:T(1024)(128)(4,1)S(1)}, s32[]{:S(2)}) async-start(s8[14254080]{0:T(1024)(128)(4,1)} %bitcast.338), calls=%async_computation.10 | async-start | bytes 8388608
  237.4 11.5 %copy-start.78 = (f32[512,3072]{1,0:T(8,128)}, f32[512,3072]{1,0:T(8,128)S(1)}, u32[]{:S(2)}) copy-start(f32[512,3072]{1,0:T(8,128)S(1)} %fusion.85) | copy-start | bytes 18874372
  237.4 11.5 %slice-start.2 = ((s8[14254080]{0:T(1024)(128)(4,1)}), s8[4194304]{0:T(1024)(128)(4,1)S(1)}, s32[]{:S(2)}) async-start(s8[14254080]{0:T(1024)(128)(4,1)} %bitcast.338), calls=%async_computation.11 | async-start | bytes 8388608
  237.4 11.5 %slice-start.3 = ((s8[14254080]{0:T(1024)(128)(4,1)}), s8[1671168]{0:T(1024)(128)(4,1)S(1)}, s32[]{:S(2)}) async-start(s8[14254080]{0:T(1024)(128)(4,1)} %bitcast.338), calls=%async_computation.12 | async-start | bytes 3342336
  483.4 409.1 %reduce-scatter.8.cloned.1.call-start = ((), (), s32[]{:S(2)}) async-start(), calls=%async_computation.6 | async-start | bytes 32292864 | tf_op jit(solution)/shard_map/reduce_scatter | solution.py:250
  591.5 6.2 copy-start.38
  592.2 7.7 copy-start.77
  597.7 7.8 slice-start.5
  599.9 5.6 copy-start.41
  611.9 312.3 %reduce-scatter.10.cloned.1.call-start = ((), (), s32[]{:S(2)}) async-start(), calls=%async_computation.8 | async-start | bytes 442368
  621.5 369.6 %all-reduce.2.cloned.1.call-start = ((), (), s32[]{:S(2)}) async-start(), calls=%async_computation.7 | async-start | bytes 3588096 | tf_op jit(solution)/shard_map/psum | solution.py:254
  896.6 9.6 copy-start.39
  906.2 28.8 %copy-start.63 = (f32[96,13]{0,1:T(8,128)S(1)}, f32[96,13]{0,1:T(8,128)}, u32[]{:S(2)}) copy-start(f32[96,13]{0,1:T(8,128)} %param.23) | copy-start | bytes 14980
  906.2 28.8 %copy-start.64 = (f32[96,13]{0,1:T(8,128)S(1)}, f32[96,13]{0,1:T(8,128)}, u32[]{:S(2)}) copy-start(f32[96,13]{0,1:T(8,128)} %param.27) | copy-start | bytes 14980
  906.3 28.8 %copy-start.65 = (f32[96,13]{0,1:T(8,128)S(1)}, f32[96,13]{0,1:T(8,128)}, u32[]{:S(2)}) copy-start(f32[96,13]{0,1:T(8,128)} %param.25) | copy-start | bytes 14980
  906.3 29.4 %copy-start.62 = (f32[96,13]{0,1:T(8,128)S(1)}, f32[96,13]{0,1:T(8,128)}, u32[]{:S(2)}) copy-start(f32[96,13]{0,1:T(8,128)} %param.29) | copy-start | bytes 14980
  935.7 64.4 %copy-start.44 = (f32[96,13]{0,1:T(8,128)}, f32[96,13]{0,1:T(8,128)S(1)}, u32[]{:S(2)}) copy-start(f32[96,13]{0,1:T(8,128)S(1)} %get-tuple-element.378) | copy-start | bytes 14980
  991.1 8.9 copy-start.32
  (71 other events, 170.4 us)
Sparse Core Ops, SparseCore 0:
  19.0 46.6 all-gather.4
  68.2 70.0 all-gather.2
  483.5 95.0 reduce-scatter.5
  612.0 280.4 reduce-scatter.7
  895.2 28.9 reduce-scatter.9
  928.2 62.9 all-reduce.1
where the time goes:
time: 1020 us; the launch traced here: 1010 us
  waiting for transfers between devices  510 us (50%)
  matrix products  282 us (28%)
  local copies, waits for them, and re-layouts  123 us (12%)
  other arithmetic  67.8 us (7%)
  between operations  16.2 us (2%)
    reduce_scatter x1, waiting for transfers between devices, on_device(): lax.psum_scatter(grad_mats, 'grp', scatter_dimension=0, tiled=True)  271 us
    dot_general x120, matrix products, precise(): jnp.dot(left, right, preferred_element_type=jnp.float32, precision=carefu...  171 us
    reduce_scatter x1, waiting for transfers between devices, on_device(): lax.psum_scatter(jnp.concatenate([d_keys_part.reshape(count, 2 * D), d_va...  87.1 us
    all_gather x1, waiting for transfers between devices, on_device(): lax.all_gather(key_feat.reshape(rows, 2 * D), 'seq', axis=0, tiled=True)  67.8 us
    psum x1, waiting for transfers between devices, on_device(): lax.psum(owned_mats.astype(jnp.bfloat16), 'seq').astype(jnp.float32)  54.8 us
    dynamic_update_slice x36, local copies, waits for them, and re-layouts, on_device(): lax.map(attend_back, (query_heads, key_heads, value_major, state_in, tota...  25.7 us
    dynamic_slice x48, local copies, waits for them, and re-layouts, on_device(): lax.map(attend_back, (query_heads, key_heads, value_major, state_in, tota...  23.5 us
    unnamed x173, local copies, waits for them, and re-layouts  23.3 us
  transfers between devices with their start and end apart: 6, of which 6 were waited for; matrix products, arithmetic and copies ran while one was open for 7% of the time, Pallas kernels for 0%

commit v1 on v0

--- a/solution.py
+++ b/solution.py
@@ -18,6 +18,32 @@
 average_keep = 0.9
 highest = lax.Precision.HIGHEST
 careful_level = lax.Precision.HIGH
+
+
+def cover_gates(vals):
+    mesh_name = "seq"
+    carry = lax.psum(1, mesh_name)
+    h_now = lax.axis_index(mesh_name)
+    lower, block_now, r2 = (carry, h_now, vals.shape[0])
+    z = tuple((h * lower if m == 0 else h for m, h in enumerate(vals.shape)))
+    raw_out = jnp.zeros(z, vals.dtype)
+    reached = lax.dynamic_update_slice_in_dim(raw_out, vals, block_now * r2, axis=0)
+    even = new = vals
+    no = 1
+    while no < lower // 2 + 1:
+        local_next = tuple(((m, (m + 1) % lower) for m in range(lower)))
+        even = lax.ppermute(even, mesh_name, local_next)
+        reached = lax.dynamic_update_slice_in_dim(
+            reached, even, (block_now - no) % lower * r2, axis=0
+        )
+        if 2 * no < lower:
+            ready = tuple(((m, (m - 1) % lower) for m in range(lower)))
+            new = lax.ppermute(new, mesh_name, ready)
+            reached = lax.dynamic_update_slice_in_dim(
+                reached, new, (block_now + no) % lower * r2, axis=0
+            )
+        no = no + 1
+    return reached
 
 
 def contract_rows(left, right):
@@ -122,7 +148,7 @@
     key_feat = key_full.astype(jnp.bfloat16)
     value_heads = values_low.reshape(rows, HEADS, HD)
     gath_keys, gath_values = (
-        lax.all_gather(key_feat.reshape(rows, 2 * D), "seq", axis=0, tiled=True),
+        cover_gates(key_feat.reshape(rows, 2 * D)),
         lax.all_gather(values_low, "seq", axis=0, tiled=True),
     )
     positions = jnp.arange(gath_keys.shape[0], dtype=jnp.int32)

time: 1020 us -> 1050 us (1.029)
  waiting for transfers between devices: 510 us -> 524 us
  local copies, waits for them, and re-layouts: 123 us -> 135 us
    ppermute x0 -> x3, waiting for transfers between devices: none -> 95.8 us  [the longest x2 77.9 us: cover_gates(): even = lax.ppermute(even, mesh_name, local_next)]
    all_gather x1 -> x0, waiting for transfers between devices: 67.8 us -> none  [on_device(): lax.all_gather(key_feat.reshape(rows, 2 * D), 'seq', axis=0, tiled=True)]
    all_gather x1, waiting for transfers between devices: 12.7 us -> 0.01 us  [on_device(): lax.all_gather(values_low, 'seq', axis=0, tiled=True)]
  transfers between devices with their start and end apart: 6 -> 8, of which waited for: 6 -> 7; matrix products, arithmetic and copies ran while one was open for 7% -> 7% of each run, Pallas kernels for 0% -> 0%
where the time goes in v1:
time: 1050 us; the launch traced here: 1040 us
  waiting for transfers between devices  524 us (50%)
  matrix products  285 us (27%)
  local copies, waits for them, and re-layouts  135 us (13%)
  other arithmetic  67.3 us (6%)
  between operations  15.9 us (2%)
    reduce_scatter x1, waiting for transfers between devices, on_device(): lax.psum_scatter(grad_mats, 'grp', scatter_dimension=0, tiled=True)  271 us
    dot_general x120, matrix products, precise(): jnp.dot(left, right, preferred_element_type=jnp.float32, precision=carefu...  170 us
    reduce_scatter x1, waiting for transfers between devices, on_device(): lax.psum_scatter(jnp.concatenate([d_keys_part.reshape(count, 2 * D), d_va...  86.2 us
    ppermute x2, waiting for transfers between devices, cover_gates(): even = lax.ppermute(even, mesh_name, local_next)  77.9 us
    psum x1, waiting for transfers between devices, on_device(): lax.psum(owned_mats.astype(jnp.bfloat16), 'seq').astype(jnp.float32)  54.8 us
    unnamed x173, local copies, waits for them, and re-layouts  26.4 us
    dynamic_update_slice x36, local copies, waits for them, and re-layouts, on_device(): lax.map(attend_back, (query_heads, key_heads, value_major, state_in, tota...  25.7 us
    dynamic_slice x48, local copies, waits for them, and re-layouts, on_device(): lax.map(attend_back, (query_heads, key_heads, value_major, state_in, tota...  23.5 us
  transfers between devices with their start and end apart: 8, of which 7 were waited for; matrix products, arithmetic and copies ran while one was open for 7% of the time, Pallas kernels for 0%

profile of v1, /device:TPU:0, one launch (start us, length us, event | category | flops | bytes accessed | tf_op | source)
XLA Modules:
  0.0 1042.9 jit_solution(13226850790410641153)
XLA Ops:
  11.6 4.2 convolution_add_fusion.3
  19.0 3.3 fusion.162
  32.5 2.9 collective-permute-start
  47.0 45.3 %collective-permute-done = bf16[512,1536]{0,1:T(8,128)(2,1)} collective-permute-done((bf16[512,1536]{0,1:T(8,128)(2,1)}, bf16[512,1536]{0,1:T(8,128)(2,1)}, u32[]{:S(2)}, u32[]{:S(2)}) %collective-permute-start) | collective-permute-done | bytes 1572896 | tf_op jit(solution)/shard_map/ppermute | solution.py:35
  96.4 2.7 copy.80
  107.3 17.9 %collective-permute-done.1 = bf16[512,1536]{0,1:T(8,128)(2,1)} collective-permute-done((bf16[512,1536]{0,1:T(8,128)(2,1)}, bf16[512,1536]{0,1:T(8,128)(2,1)}, u32[]{:S(2)}, u32[]{:S(2)}) %collective-permute-start.1) | collective-permute-done | bytes 1572896 | tf_op jit(solution)/shard_map/ppermute | solution.py:41
  126.9 32.6 %collective-permute-done.2 = bf16[512,1536]{0,1:T(8,128)(2,1)} collective-permute-done((bf16[512,1536]{0,1:T(8,128)(2,1)}, bf16[512,1536]{0,1:T(8,128)(2,1)}, u32[]{:S(2)}, u32[]{:S(2)}) %collective-permute-start.2) | collective-permute-done | bytes 1572896 | tf_op jit(solution)/shard_map/ppermute | solution.py:35
  163.8 4.7 convert_reduce_fusion
  168.4 4.6 copy.78
  173.1 5.5 fusion.171
  179.9 81.3 %while.33 = (s32[]{:T(128)}, f32[12,512,64]{1,2,0:T(8,128)}, f32[12,512]{1,0:T(8,128)}, bf16[12,512,128]{2,1,0:T(8,128)(2,1)}, bf16[12,512,128]{2,1,0:T(8,128)(2...) while((s32[]{:T(128)}, f32[12,512,64]{1,2,0:T(8,128)}, ...), condition=%wide.region_13.14_spmd.clone, body=%wide.region_11.13_spmd.clone.sunk | while | flops 194183168 | bytes 3231861 | solution.py:178
  265.9 5.0 fusion.85
  271.0 10.9 %convert_reduce_fusion.1 = (f32[3072]{0:T(1024)}, bf16[512,3072]{1,0:T(8,128)(2,1)S(1)}) fusion(f32[512,3072]{1,0:T(8,128)S(1)} %fusion.85, f32[3072]{0:T(1024)S(1)} %add.251, bf16[512,768]{1,0:T(8,128)(2,1)S(1)} %copy-done.40, bf16[768,9280]{0,1:T(8,128)(2,1)} %param.20), kind=kOutput, calls=%fused_computation.105 | convolution fusion | flops 2452091904 | bytes 14966784 | tf_op jit(solution)/shard_map/dot_general | solution.py:191
  282.0 3.5 multiply_reduce_fusion
  291.6 203.7 %while.34 = (s32[]{:T(128)}, f32[12,512,128]{1,2,0:T(8,128)}, f32[12,512,128]{1,2,0:T(8,128)}, f32[12,512,64]{1,2,0:T(8,128)}, f32[12,128,64]{1,2,0:T(8,128)}, /...) while((s32[]{:T(128)}, f32[12,512,128]{1,2,0:T(8,128)}, ...), condition=%wide.region_20.21_spmd.clone.clone, body=%wide.region_18.20_spmd.clone.clone.sunk | while | flops 723526784 | bytes 10363109 | solution.py:223
  495.3 5.1 multiply_convert_fusion.1
  500.5 5.4 multiply_convert_fusion
  505.8 11.6 %pad_maximum_fusion = bf16[2048,2304]{0,1:T(8,128)(2,1)} fusion(bf16[2048,768]{0,1:T(8,128)(2,1)S(1)} %bitcast.307, bf16[2048,1536]{0,1:T(8,128)(2,1)S(1)} %bitcast.302), kind=kLoop, calls=%fused_computation.92 | loop fusion | flops 18874368 | bytes 18874368 | tf_op jit(solution)/shard_map/concatenate | solution.py:240
  518.9 3.4 multiply_reduce_fusion.4
  525.6 86.2 %reduce-scatter.6.cloned.1.call-done = bf16[512,2304]{0,1:T(8,128)(2,1)} async-done(((bf16[2048,2304]{0,1:T(8,128)(2,1)}), bf16[512,2304]{0,1:T(8,128)(2,1)}) %reduce-scatter.6.cloned.1.call-update) | async-done | bytes 2359312 | tf_op jit(solution)/shard_map/reduce_scatter | solution.py:239
  625.4 5.4 convolution_dynamic-update-slice_fusion
  633.1 5.5 convolution_dynamic-update-slice_fusion.1
  638.7 5.5 bitcast_dynamic-update-slice_fusion
  647.6 6.0 fusion.110
  655.0 270.6 %reduce-scatter.8.cloned.1.call-done = f32[96,9280]{1,0:T(8,128)} async-done(((f32[768,9280]{1,0:T(8,128)}), f32[96,9280]{1,0:T(8,128)}) %reduce-scatter.8.cloned.1.call-update) | async-done | bytes 3563536 | tf_op jit(solution)/shard_map/reduce_scatter | solution.py:276
  925.6 3.4 convert_element_type.146
  929.8 9.6 add_convert_fusion
  940.9 16.5 %reduce-scatter.10.cloned.1.call-done = f32[96,13]{1,0:T(8,128)} async-done(((f32[768,13]{1,0:T(8,128)}), f32[96,13]{1,0:T(8,128)}) %reduce-scatter.10.cloned.1.call-update) | async-done | bytes 5008
  958.3 9.9 psum.15
  969.4 54.8 %all-reduce.2.cloned.1.call-done = bf16[96,9280]{1,0:T(8,128)(2,1)} async-done(((bf16[96,9280]{1,0:T(8,128)(2,1)}), bf16[96,9280]{1,0:T(8,128)(2,1)}) %all-reduce.2.cloned.1.call-update) | async-done | bytes 1781776 | tf_op jit(solution)/shard_map/psum | solution.py:280
  1024.2 8.9 fusion.158
  1033.1 2.8 multiply_add_fusion.1
  (585 shorter events, 372.2 us)
Async XLA Ops:
  7.2 161.2 %all-gather.2.cloned.1.call-start = ((), (), s32[]{:S(2)}) async-start(), calls=%async_computation.3 | async-start | bytes 3932160 | tf_op jit(solution)/shard_map/all_gather | solution.py:152
  8.7 7.1 copy-start.53
  8.7 7.1 copy-start.71
  8.7 257.2 %copy-start.69 = (f32[768]{0:T(1024)}, f32[768]{0:T(1024)S(1)}, u32[]{:S(2)}) copy-start(f32[768]{0:T(1024)S(1)} %get-tuple-element.327) | copy-start | bytes 9220
  8.7 276.8 %copy-start.51 = (f32[768]{0:T(1024)}, f32[768]{0:T(1024)S(1)}, u32[]{:S(2)}) copy-start(f32[768]{0:T(1024)S(1)} %get-tuple-element.325) | copy-start | bytes 9220
  18.9 592.8 %reduce-scatter.6.cloned.1.call-start = ((), (), s32[]{:S(2)}) async-start(), calls=%async_computation.4 | async-start | bytes 11796480 | tf_op jit(solution)/shard_map/reduce_scatter | solution.py:239
  22.4 17.7 %copy-start.30 = (bf16[768,64]{1,0:T(8,128)(2,1)}, bf16[768,64]{1,0:T(8,128)(2,1)S(1)}, u32[]{:S(2)}) copy-start(bf16[768,64]{1,0:T(8,128)(2,1)S(1)} %copy.136) | copy-start | bytes 294916
  30.8 6.3 copy-start.19
  32.5 59.9 %collective-permute-start = (bf16[512,1536]{0,1:T(8,128)(2,1)}, bf16[512,1536]{0,1:T(8,128)(2,1)}, u32[]{:S(2)}, u32[]{:S(2)}) collective-permute-start(bf16[512,1536]{0,1:T(8,128)(2,1)} %bitcast.9), channel_id=1, source_target_pairs={{0,8},{8,16},{16,24},{24,0},{1,9},{9,17},{17,25},{25,1},{2,10},{10... | collective-permute-start | bytes 4718600 | tf_op jit(solution)/shard_map/ppermute | solution.py:35
  35.4 89.8 %collective-permute-start.1 = (bf16[512,1536]{0,1:T(8,128)(2,1)}, bf16[512,1536]{0,1:T(8,128)(2,1)}, u32[]{:S(2)}, u32[]{:S(2)}) collective-permute-start(bf16[512,1536]{0,1:T(8,128)(2,1)} %bitcast.9), channel_id=1, source_target_pairs={{0,24},{8,0},{16,8},{24,16},{1,25},{9,1},{17,9},{25,17},{2,26},{10... | collective-permute-start | bytes 4718600 | tf_op jit(solution)/shard_map/ppermute | solution.py:41
  92.3 67.1 %collective-permute-start.2 = (bf16[512,1536]{0,1:T(8,128)(2,1)}, bf16[512,1536]{0,1:T(8,128)(2,1)}, u32[]{:S(2)}, u32[]{:S(2)}) collective-permute-start(bf16[512,1536]{0,1:T(8,128)(2,1)} %collective-permute-done), channel_id=1, source_target_pairs={{0,8},{8,16},{16,24},{24,0},{1,9},{9,17},{17,25},{25,1},{2,10},{10... | collective-permute-start | bytes 4718600 | tf_op jit(solution)/shard_map/ppermute | solution.py:35
  92.5 178.4 %copy-start.55 = (f32[3072]{0:T(1024)}, f32[3072]{0:T(1024)S(1)}, u32[]{:S(2)}) copy-start(f32[3072]{0:T(1024)S(1)} %add.251) | copy-start | bytes 36868
  265.5 20.0 %copy-start.27 = (f32[512,768]{1,0:T(8,128)}, f32[512,768]{1,0:T(8,128)S(1)}, u32[]{:S(2)}) copy-start(f32[512,768]{1,0:T(8,128)S(1)} %get-tuple-element.409) | copy-start | bytes 4718596
  265.6 19.9 %copy-start.47 = (f32[512]{0:T(512)}, f32[512]{0:T(512)S(1)}, u32[]{:S(2)}) copy-start(f32[512]{0:T(512)S(1)} %broadcast_multiply_fusion.5) | copy-start | bytes 6148
  265.9 19.6 %copy-start.60 = (f32[512]{0:T(512)}, f32[512]{0:T(512)S(1)}, u32[]{:S(2)}) copy-start(f32[512]{0:T(512)S(1)} %add_rsqrt_fusion) | copy-start | bytes 6148
  265.9 16.0 %slice-start = ((s8[14254080]{0:T(1024)(128)(4,1)}), s8[4194304]{0:T(1024)(128)(4,1)S(1)}, s32[]{:S(2)}) async-start(s8[14254080]{0:T(1024)(128)(4,1)} %bitcast.337), calls=%async_computation.8 | async-start | bytes 8388608
  265.9 16.0 %slice-start.1 = ((s8[14254080]{0:T(1024)(128)(4,1)}), s8[4194304]{0:T(1024)(128)(4,1)S(1)}, s32[]{:S(2)}) async-start(s8[14254080]{0:T(1024)(128)(4,1)} %bitcast.337), calls=%async_computation.9 | async-start | bytes 8388608
  271.0 11.0 %copy-start.78 = (f32[512,3072]{1,0:T(8,128)}, f32[512,3072]{1,0:T(8,128)S(1)}, u32[]{:S(2)}) copy-start(f32[512,3072]{1,0:T(8,128)S(1)} %fusion.85) | copy-start | bytes 18874372
  271.0 11.0 %slice-start.2 = ((s8[14254080]{0:T(1024)(128)(4,1)}), s8[4194304]{0:T(1024)(128)(4,1)S(1)}, s32[]{:S(2)}) async-start(s8[14254080]{0:T(1024)(128)(4,1)} %bitcast.337), calls=%async_computation.10 | async-start | bytes 8388608
  271.0 11.0 %slice-start.3 = ((s8[14254080]{0:T(1024)(128)(4,1)}), s8[1671168]{0:T(1024)(128)(4,1)S(1)}, s32[]{:S(2)}) async-start(s8[14254080]{0:T(1024)(128)(4,1)} %bitcast.337), calls=%async_computation.11 | async-start | bytes 3342336
  517.5 408.2 %reduce-scatter.8.cloned.1.call-start = ((), (), s32[]{:S(2)}) async-start(), calls=%async_computation.5 | async-start | bytes 32292864 | tf_op jit(solution)/shard_map/reduce_scatter | solution.py:276
  625.4 7.7 copy-start.77
  630.8 7.8 slice-start.5
  645.0 312.4 %reduce-scatter.10.cloned.1.call-start = ((), (), s32[]{:S(2)}) async-start(), calls=%async_computation.7 | async-start | bytes 442368
  654.7 369.5 %all-reduce.2.cloned.1.call-start = ((), (), s32[]{:S(2)}) async-start(), calls=%async_computation.6 | async-start | bytes 3588096 | tf_op jit(solution)/shard_map/psum | solution.py:280
  929.8 9.6 copy-start.39
  939.4 28.7 %copy-start.63 = (f32[96,13]{0,1:T(8,128)S(1)}, f32[96,13]{0,1:T(8,128)}, u32[]{:S(2)}) copy-start(f32[96,13]{0,1:T(8,128)} %param.23) | copy-start | bytes 14980
  939.4 28.7 %copy-start.64 = (f32[96,13]{0,1:T(8,128)S(1)}, f32[96,13]{0,1:T(8,128)}, u32[]{:S(2)}) copy-start(f32[96,13]{0,1:T(8,128)} %param.27) | copy-start | bytes 14980
  939.4 28.7 %copy-start.65 = (f32[96,13]{0,1:T(8,128)S(1)}, f32[96,13]{0,1:T(8,128)}, u32[]{:S(2)}) copy-start(f32[96,13]{0,1:T(8,128)} %param.25) | copy-start | bytes 14980
  939.4 29.4 %copy-start.62 = (f32[96,13]{0,1:T(8,128)S(1)}, f32[96,13]{0,1:T(8,128)}, u32[]{:S(2)}) copy-start(f32[96,13]{0,1:T(8,128)} %param.29) | copy-start | bytes 14980
  968.8 64.3 %copy-start.44 = (f32[96,13]{0,1:T(8,128)}, f32[96,13]{0,1:T(8,128)S(1)}, u32[]{:S(2)}) copy-start(f32[96,13]{0,1:T(8,128)S(1)} %get-tuple-element.378) | copy-start | bytes 14980
  1024.2 8.9 copy-start.32
  (73 other events, 185.7 us)
Sparse Core Ops, SparseCore 0:
  19.0 67.7 all-gather.1
  517.6 94.1 reduce-scatter.5
  645.2 280.4 reduce-scatter.7
  928.3 29.0 reduce-scatter.9
  961.4 62.7 all-reduce.1
